TPU v7x, 32 devices: a whole 2x2x4 slice. The times are simulated.
32 devices in a mesh: cand: 4 (over x, core), seq: 8 (over z, y).
Axes of the slice: x: 2, y: 2, z: 4, core: 2. Of those that a mesh axis runs over, the one named last changes fastest.
Arguments:
- latent: bfloat16 [4, 384, 3072], P('cand', 'seq'), may hold values from -0.59765625 to 0.59765625
- timesteps: int32 [4], replicated, may hold values from 0 to 999
- positions: int32 [3, 384], replicated, may hold values from 0 to 63
- mod_weight: bfloat16 [3072, 9216], P('cand', 'seq'), may hold values from -0.109375 to 0.109375
- input_weight: bfloat16 [3072, 16, 384], P('cand', 'seq'), may hold values from -0.109375 to 0.109375
- output_weight: bfloat16 [16, 128, 3072], P('seq', None, 'cand'), may hold values from -0.75 to 0.75
- cotangent: bfloat16 [4, 384, 3072], P('cand', 'seq'), may hold values from -6 to 6
Outputs:
- block_out: bfloat16 [4, 384, 3072], P('cand', 'seq')
- latent_grad: float32 [4, 384, 3072], P('cand', 'seq')
All inputs are finite; a program needn't handle non-finite values.
Results may differ from a plain program's by a relative error of at most 0.033.
Values may be sent and summed in bfloat16 or wider, within the bound.
A program may use at most 128 MiB of HBM per device.

v0:
```python
import jax
import jax.numpy as jnp
import numpy as np
from jax import lax
from jax.sharding import PartitionSpec as P

HEAD = 128
epsilon = 1e-06


def time_embed(timesteps, feature_width):
    half_size = feature_width // 2
    freq_rate = jnp.exp(-jnp.log(10000.0) * jnp.arange(half_size, dtype=jnp.float32) / half_size)
    angles = timesteps.astype(jnp.float32)[:, None] * freq_rate[None, :]
    return jnp.concatenate([jnp.cos(angles), jnp.sin(angles)], axis=1)


def rope_tables(positions, head_size):
    first_size = head_size // 8
    other_size = (head_size - first_size) // 2
    pieces = []
    swapped = []
    sign_vec = []
    offset = 0
    for axis_id, width_part in enumerate((first_size, other_size, other_size)):
        half_size = width_part // 2
        freq_rate = jnp.exp(
            -jnp.log(256.0) * 2.0 * jnp.arange(half_size, dtype=jnp.float32) / width_part
        )
        angle_part = positions[axis_id].astype(jnp.float32)[:, None] * freq_rate[None, :]
        pieces.append(angle_part)
        pieces.append(angle_part)
        swapped += list(range(offset + half_size, offset + width_part)) + list(
            range(offset, offset + half_size)
        )
        sign_vec += [-1.0] * half_size + [1.0] * half_size
        offset += width_part
    angles = jnp.concatenate(pieces, axis=1)
    return (
        jnp.cos(angles),
        jnp.sin(angles),
        np.array(swapped, np.int32),
        np.array(sign_vec, np.float32),
    )


def rotate(values, tables):
    cos_tab, sin_tab, swapped, sign_vec = tables
    return values * cos_tab + values[..., swapped] * sign_vec * sin_tab


def unrotate(values, tables):
    cos_tab, sin_tab, swapped, sign_vec = tables
    return values * cos_tab - (values * sin_tab)[..., swapped] * sign_vec


def rms_norm(values):
    inverse = lax.rsqrt(jnp.mean(values * values, -1, keepdims=True) + epsilon)
    return (values * inverse, inverse)


def rms_back(d_normed, normed, inverse):
    return inverse * (d_normed - normed * jnp.mean(d_normed * normed, -1, keepdims=True))


def layer_norm(values):
    centred = values - jnp.mean(values, -1, keepdims=True)
    inverse_std = lax.rsqrt(jnp.mean(centred * centred, -1, keepdims=True) + epsilon)
    return (centred * inverse_std, inverse_std)


def layer_norm_back(d_normed, normed, inverse_std):
    return inverse_std * (
        d_normed
        - jnp.mean(d_normed, -1, keepdims=True)
        - normed * jnp.mean(d_normed * normed, -1, keepdims=True)
    )


def times_transposed(left, right):
    return lax.dot_general(
        left, right, (((1,), (1,)), ((), ())), preferred_element_type=jnp.float32
    )


def attend(projected, tables):
    length, groups, triple = projected.shape
    head_size = triple // 3
    grouped = jnp.transpose(projected.reshape(length, groups, 3, head_size), (2, 1, 0, 3))
    query_n, query_inv = rms_norm(grouped[0])
    key_n, key_inv = rms_norm(grouped[1])
    q_rot = rotate(query_n, tables).astype(jnp.bfloat16)
    k_rot = rotate(key_n, tables).astype(jnp.bfloat16)
    values = grouped[2].astype(jnp.bfloat16)
    score_scale = head_size ** (-0.5)
    scores = (
        jnp.einsum("gld,gmd->glm", q_rot, k_rot, preferred_element_type=jnp.float32) * score_scale
    )
    weights = jnp.exp(scores - head_size**0.5)
    probs = weights / jnp.sum(weights, -1, keepdims=True)
    probs_low = probs.astype(jnp.bfloat16)
    heads_out = jnp.einsum("glm,gmd->gld", probs_low, values, preferred_element_type=jnp.float32)
    attended = (
        jnp.transpose(heads_out, (1, 0, 2)).reshape(length, groups * head_size).astype(jnp.bfloat16)
    )
    saved = (q_rot, k_rot, values, probs, probs_low, query_n, query_inv, key_n, key_inv)
    return (attended, saved)


def attend_back(d_attended, saved, tables):
    q_rot, k_rot, values, probs, probs_low, query_n, query_inv, key_n, key_inv = saved
    groups, length, head_size = q_rot.shape
    score_scale = head_size ** (-0.5)
    d_heads = jnp.transpose(d_attended.reshape(length, groups, head_size), (1, 0, 2))
    d_values = jnp.einsum("glm,gld->gmd", probs_low, d_heads, preferred_element_type=jnp.float32)
    d_probs = jnp.einsum("gld,gmd->glm", d_heads, values, preferred_element_type=jnp.float32)
    d_scores = (probs * (d_probs - jnp.sum(probs * d_probs, -1, keepdims=True))).astype(
        jnp.bfloat16
    )
    d_qrot = (
        jnp.einsum("glm,gmd->gld", d_scores, k_rot, preferred_element_type=jnp.float32)
        * score_scale
    )
    d_krot = (
        jnp.einsum("glm,gld->gmd", d_scores, q_rot, preferred_element_type=jnp.float32)
        * score_scale
    )
    d_query = rms_back(unrotate(d_qrot, tables), query_n, query_inv)
    d_key = rms_back(unrotate(d_krot, tables), key_n, key_inv)
    stacked = jnp.stack([d_query, d_key, d_values], 0)
    return (
        jnp.transpose(stacked, (2, 1, 0, 3))
        .reshape(length, groups * 3 * head_size)
        .astype(jnp.bfloat16)
    )


def on_device(latent, timesteps, positions, mod_weight, input_weight, output_weight, cotangent):
    width = latent.shape[2]
    rows_local = latent.shape[1]
    groups = input_weight.shape[1]
    group_cols = groups * input_weight.shape[2]
    time_act = jax.nn.silu(time_embed(timesteps, width)).astype(jnp.bfloat16)
    slab_rows = mod_weight.shape[0]
    act_rows = lax.dynamic_slice_in_dim(time_act, lax.axis_index("cand") * slab_rows, slab_rows, 1)
    mod_mine = lax.psum_scatter(
        jnp.dot(act_rows, mod_weight, preferred_element_type=jnp.float32).astype(jnp.bfloat16),
        "cand",
        scatter_dimension=0,
        tiled=True,
    ).astype(jnp.float32)
    modulation = lax.all_gather(mod_mine, "seq", axis=1, tiled=True)[0]
    shift_vec = modulation[:width]
    scale_vec = modulation[width : 2 * width]
    gate_vec = modulation[2 * width :]
    latent_rows = latent[0].astype(jnp.float32)
    normed, inverse_std = layer_norm(latent_rows)
    modulated = (normed * (1.0 + scale_vec) + shift_vec).astype(jnp.bfloat16)
    gathered = lax.all_gather(modulated, "seq", axis=0, tiled=True)
    length = gathered.shape[0]
    tables = rope_tables(positions, HEAD)
    piece = lax.all_gather(input_weight, "cand", axis=0, tiled=True)
    projected = jnp.dot(
        gathered, piece.reshape(piece.shape[0], group_cols), preferred_element_type=jnp.float32
    )
    attended, saved = attend(projected.reshape(length, groups, 3 * HEAD), tables)
    w_heads = lax.all_gather(output_weight, "seq", axis=0, tiled=True)
    w_all = lax.all_gather(w_heads, "cand", axis=2, tiled=True)
    w_all = w_all.reshape(w_all.shape[0] * w_all.shape[1], width)
    token_heads = lax.all_to_all(attended, "seq", split_axis=0, concat_axis=1, tiled=True)
    mixed = jnp.dot(token_heads, w_all, preferred_element_type=jnp.float32)
    block_out = (latent_rows + gate_vec * mixed).astype(jnp.bfloat16)
    d_mixed = (cotangent[0].astype(jnp.float32) * gate_vec).astype(jnp.bfloat16)
    d_tokens = times_transposed(d_mixed, w_all).astype(jnp.bfloat16)
    d_attended = lax.all_to_all(d_tokens, "seq", split_axis=1, concat_axis=0, tiled=True)
    d_projected = attend_back(d_attended, saved, tables)
    w_back = lax.all_gather(input_weight, "cand", axis=0, tiled=True).reshape(width, group_cols)
    d_modulated = lax.psum_scatter(
        times_transposed(
            lax.slice_in_dim(d_projected, 0, rows_local * lax.axis_size("seq"), axis=0), w_back
        ).astype(jnp.bfloat16),
        "seq",
        scatter_dimension=0,
        tiled=True,
    ).astype(jnp.float32)
    latent_grad = cotangent[0].astype(jnp.float32) + layer_norm_back(
        d_modulated * (1.0 + scale_vec), normed, inverse_std
    )
    return (block_out[None], latent_grad[None])


def solution(mesh):
    placed = (
        P("cand", "seq", None),
        P(),
        P(),
        P("cand", "seq"),
        P("cand", "seq", None),
        P("seq", None, "cand"),
        P("cand", "seq", None),
    )
    return jax.shard_map(
        on_device,
        mesh=mesh,
        in_specs=placed,
        out_specs=(P("cand", "seq", None), P("cand", "seq", None)),
        check_vma=False,
    )
```

profile of v0, /device:TPU:0, one launch (start us, length us, event | category | flops | bytes accessed | tf_op | source)
XLA Modules:
  0.0 380.3 jit_solution(16041550091423698796)
XLA Ops:
  10.0 8.7 %all-reduce = bf16[4,1152]{1,0:T(4,128)(2,1)S(1)} all-reduce(bf16[4,1152]{1,0:T(4,128)(2,1)S(1)} %convolution_convert_fusion.2), channel_id=2, replica_groups=mesh['cand'=4,'seq'=8] {'cand'}, use_global_device_ids=true, to_apply=%region_0.1.clone | all-reduce | flops 4608 | bytes 18432
  19.4 31.6 %all_gather.16 = f32[1,9216]{1,0:T(1,128)S(1)} all-gather(f32[1,1152]{1,0:T(1,128)S(1)} %dynamic-slice_convert_fusion), channel_id=1, replica_groups=mesh['cand'=4,'seq'=8] {'seq'}, dimensions={1}, use_global_device_ids=true | all-gather | bytes 41472 | tf_op jit(solution)/shard_map/all_gather | solution.py:152
  52.4 20.8 %all-gather.9.cloned.1.call-done = bf16[16,128,768]{2,1,0:T(8,128)(2,1)} async-done(((bf16[2,128,768]{2,1,0:T(8,128)(2,1)}), bf16[16,128,768]{2,1,0:T(8,128)(2,1)}) %all-gather.9.cloned.1.call-update) | async-done | bytes 3145744 | tf_op jit(solution)/shard_map/all_gather | solution.py:167
  76.4 34.5 %all-gather.7.cloned.1.call-done = bf16[3072,2,384]{2,1,0:T(2,128)(2,1)} async-done(((bf16[768,2,384]{2,1,0:T(2,128)(2,1)}), bf16[3072,2,384]{2,1,0:T(2,128)(2,1)}) %all-gather.7.cloned.1.call-update) | async-done | bytes 4718608 | tf_op jit(solution)/shard_map/all_gather | solution.py:162
  110.9 5.2 %copy.89 = bf16[384,8,2,384]{3,1,2,0:T(8,128)(2,1)} copy(bf16[384,8,2,384]{3,2,1,0:T(2,128)(2,1)} %bitcast.149) | data formatting | bytes 9437184
  116.1 6.7 %copy.50 = bf16[3072,768]{0,1:T(8,128)(2,1)} copy(bf16[3072,768]{1,0:T(8,128)(2,1)} %bitcast.145) | data formatting | bytes 9437184 | tf_op jit(solution)/shard_map/reshape | solution.py:164
  122.8 42.7 %all-gather.5.cloned.1.call-done = bf16[384,3072]{1,0:T(8,128)(2,1)} async-done(((bf16[48,3072]{1,0:T(8,128)(2,1)}), bf16[384,3072]{1,0:T(8,128)(2,1)}) %all-gather.5.cloned.1.call-update) | async-done | bytes 2359312 | tf_op jit(solution)/shard_map/all_gather | solution.py:159
  165.5 5.3 %fusion.5 = f32[3,2,384,128]{2,3,0,1:T(8,128)S(1)} fusion(bf16[2,3,128,3072]{3,2,1,0:T(8,128)(2,1)} %bitcast.150, bf16[384,3072]{1,0:T(8,128)(2,1)} %all-gather.5.cloned.1.call-done), kind=kOutput, calls=%fused_computation.13 | convolution fusion | flops 1811939328 | bytes 8257536 | tf_op jit(solution)/shard_map/dot_general | solution.py:163
  171.9 75.6 %all-gather.11.cloned.1.call-done = bf16[16,128,3072]{2,1,0:T(8,128)(2,1)} async-done(((bf16[16,128,768]{2,1,0:T(8,128)(2,1)}), bf16[16,128,3072]{2,1,0:T(8,128)(2,1)}) %all-gather.11.cloned.1.call-update) | async-done | bytes 12582928 | tf_op jit(solution)/shard_map/all_gather | solution.py:168
  247.6 8.5 %convolution_convert_fusion.1 = bf16[48,2048]{1,0:T(8,128)(2,1)S(1)} fusion(bf16[2048,3072]{1,0:T(8,128)(2,1)} %bitcast.143, bf16[1,48,3072]{2,1,0:T(8,128)(2,1)S(1)} %copy-done.10, f32[3072]{0:T(1024)S(1)} %bitcast.159), kind=kOutput, calls=%fused_computation.11 | convolution fusion | flops 604520448 | bytes 13086720 | tf_op jit(solution)/shard_map/dot_general | solution.py:81
  256.7 5.5 %all-to-all-start.1 = ((bf16[48,8,256]{2,0,1:T(8,128)(2,1)}), bf16[48,8,256]{2,0,1:T(8,128)(2,1)S(1)}, u32[]{:S(2)}, u32[]{:S(2)}) async-start(bf16[48,8,256]{2,0,1:T(8,128)(2,1)} %bitcast.142), calls=%async_computation.1 | async-start | bytes 393216 | tf_op jit(solution)/shard_map/all_to_all | solution.py:175
  262.5 1.2 fusion.35
  263.7 1.1 copy.52
  265.8 2.2 gather_fusion
  268.0 2.9 gather_fusion.1
  270.9 1.9 fusion.31
  272.9 2.5 fusion.45
  275.3 2.1 multiply_reduce_fusion
  277.5 1.1 fusion.11
  280.7 1.1 broadcast_multiply_fusion
  282.8 2.9 gather_fusion.3
  285.7 2.0 copy.66
  287.8 2.9 gather_fusion.2
  290.6 2.0 multiply_reduce_fusion.2
  292.7 2.0 fusion.41
  294.9 3.5 convolution_convert_fusion
  298.4 1.4 fusion.10
  300.2 18.7 %all_to_all.32 = bf16[8,48,256]{2,1,0:T(8,128)(2,1)S(1)} all-to-all(bf16[8,48,256]{2,1,0:T(8,128)(2,1)S(1)} %convert_element_type.131), channel_id=1, replica_groups=mesh['cand'=4,'seq'=8] {'seq'}, dimensions={0} | all-to-all | bytes 393216 | tf_op jit(solution)/shard_map/all_to_all | solution.py:170
  319.0 7.9 %fusion.2 = bf16[1,48,3072]{2,1,0:T(8,128)(2,1)} fusion(bf16[48,2048]{1,0:T(8,128)(2,1)S(1)} %bitcast.151, bf16[2048,3072]{1,0:T(8,128)(2,1)} %bitcast.144, bf16[1,48,3072]{2,1,0:T(8,128)(2,1)S(1)} %copy-done.2, f32[3072]{0:T(1024)S(1)} %bitcast.160), kind=kOutput, calls=%fused_computation.8 | convolution fusion | flops 604569600 | bytes 13381632 | tf_op jit(solution)/shard_map/dot_general | solution.py:171
  326.9 43.6 %reduce-scatter.2.cloned.1.call-done = bf16[48,3072]{1,0:T(8,128)(2,1)} async-done(((bf16[384,3072]{1,0:T(8,128)(2,1)}), bf16[48,3072]{1,0:T(8,128)(2,1)}) %reduce-scatter.2.cloned.1.call-update) | async-done | bytes 294928 | tf_op jit(solution)/shard_map/reduce_scatter | solution.py:178
  370.5 1.2 fusion.27
  371.8 2.0 fusion.24
  (112 shorter events, 14.9 us)
Async XLA Ops:
  7.2 2.5 copy-start
  7.2 1.6 copy-start.28
  7.2 1.6 copy-start.27
  7.2 66.0 %all-gather.9.cloned.1.call-start = ((), (), s32[]{:S(2)}) async-start(), calls=%async_computation.5 | async-start | bytes 3538944 | tf_op jit(solution)/shard_map/all_gather | solution.py:167
  7.9 103.0 %all-gather.7.cloned.1.call-start = ((), (), s32[]{:S(2)}) async-start(), calls=%async_computation.4 | async-start | bytes 5898240 | tf_op jit(solution)/shard_map/all_gather | solution.py:162
  8.7 42.3 %copy-start.1 = (bf16[1,48,3072]{2,1,0:T(8,128)(2,1)S(1)}, bf16[1,48,3072]{2,1,0:T(8,128)(2,1)}, u32[]{:S(2)}) copy-start(bf16[1,48,3072]{2,1,0:T(8,128)(2,1)} %param.13) | copy-start | bytes 884740
  8.7 156.8 %all-gather.5.cloned.1.call-start = ((), (), s32[]{:S(2)}) async-start(), calls=%async_computation.3 | async-start | bytes 2654208 | tf_op jit(solution)/shard_map/all_gather | solution.py:159
  51.1 22.1 %copy-start.20 = (f32[48]{0:T(128)}, f32[48]{0:T(128)S(1)}, u32[]{:S(2)}) copy-start(f32[48]{0:T(128)S(1)} %broadcast_multiply_fusion.11) | copy-start | bytes 580
  51.4 21.8 %copy-start.23 = (f32[48]{0:T(128)}, f32[48]{0:T(128)S(1)}, u32[]{:S(2)}) copy-start(f32[48]{0:T(128)S(1)} %add_rsqrt_fusion.2) | copy-start | bytes 580
  51.4 196.1 %copy-start.16 = (f32[1,3072]{1,0:T(1,128)}, f32[1,3072]{1,0:T(1,128)S(1)}, u32[]{:S(2)}) copy-start(f32[1,3072]{1,0:T(1,128)S(1)} %get-tuple-element.21) | copy-start | bytes 36868
  52.4 195.2 %all-gather.11.cloned.1.call-start = ((), (), s32[]{:S(2)}) async-start(), calls=%async_computation.6 | async-start | bytes 15728640 | tf_op jit(solution)/shard_map/all_gather | solution.py:168
  73.2 1.2 copy-start.26
  165.5 82.1 %copy-start.10 = (bf16[1,48,3072]{2,1,0:T(8,128)(2,1)S(1)}, bf16[1,48,3072]{2,1,0:T(8,128)(2,1)}, u32[]{:S(2)}) copy-start(bf16[1,48,3072]{2,1,0:T(8,128)(2,1)} %param.19) | copy-start | bytes 884740
  171.9 90.5 %copy-start.18 = (f32[2,384]{1,0:T(2,128)}, f32[2,384]{1,0:T(2,128)S(1)}, u32[]{:S(2)}) copy-start(f32[2,384]{1,0:T(2,128)S(1)} %get-tuple-element.32) | copy-start | bytes 9220
  256.7 16.1 %all-to-all-start.1 = ((bf16[48,8,256]{2,0,1:T(8,128)(2,1)}), bf16[48,8,256]{2,0,1:T(8,128)(2,1)S(1)}, u32[]{:S(2)}, u32[]{:S(2)}) async-start(bf16[48,8,256]{2,0,1:T(8,128)(2,1)} %bitcast.142), calls=%async_computation.1 | async-start | bytes 393216 | tf_op jit(solution)/shard_map/all_to_all | solution.py:175
  262.2 108.2 %reduce-scatter.2.cloned.1.call-start = ((), (), s32[]{:S(2)}) async-start(), calls=%async_computation.7 | async-start | bytes 2654208 | tf_op jit(solution)/shard_map/reduce_scatter | solution.py:178
  263.7 11.7 %copy-start.3 = (f32[2,384,128]{1,2,0:T(8,128)}, f32[2,384,128]{1,2,0:T(8,128)S(1)}, u32[]{:S(2)}) copy-start(f32[2,384,128]{1,2,0:T(8,128)S(1)} %get-tuple-element.11) | copy-start | bytes 1179652
  263.7 11.7 %copy-start.4 = (f32[2,384,128]{1,2,0:T(8,128)}, f32[2,384,128]{1,2,0:T(8,128)S(1)}, u32[]{:S(2)}) copy-start(f32[2,384,128]{1,2,0:T(8,128)S(1)} %get-tuple-element.12) | copy-start | bytes 1179652
  272.8 2.5 copy-start.8
  275.3 2.1 copy-start.9
  277.5 1.3 copy-start.7
  279.9 1.9 copy-start.5
  281.8 13.1 %slice-start = ((s8[4718592]{0:T(1024)(128)(4,1)}), s8[524288]{0:T(1024)(128)(4,1)S(1)}, s32[]{:S(2)}) async-start(s8[4718592]{0:T(1024)(128)(4,1)} %bitcast.146), calls=%async_computation.8 | async-start | bytes 1048576
  282.8 7.8 %copy-start.22 = (f32[128]{0:T(128)S(1)}, f32[128]{0:T(128)}, u32[]{:S(2)}) copy-start(f32[128]{0:T(128)} %constant.63.clone) | copy-start | bytes 1540
  287.8 4.9 %copy-start.19 = (f32[2,384]{1,0:T(2,128)S(1)}, f32[2,384]{1,0:T(2,128)}, u32[]{:S(2)}) copy-start(f32[2,384]{1,0:T(2,128)} %copy-done.18) | copy-start | bytes 9220
  290.6 4.2 %slice-start.1 = ((s8[4718592]{0:T(1024)(128)(4,1)}), s8[4194304]{0:T(1024)(128)(4,1)S(1)}, s32[]{:S(2)}) async-start(s8[4718592]{0:T(1024)(128)(4,1)} %bitcast.146), calls=%async_computation.9 | async-start | bytes 8388608
  292.7 2.0 copy-start.12
  299.8 19.1 %copy-start.2 = (bf16[1,48,3072]{2,1,0:T(8,128)(2,1)S(1)}, bf16[1,48,3072]{2,1,0:T(8,128)(2,1)}, u32[]{:S(2)}) copy-start(bf16[1,48,3072]{2,1,0:T(8,128)(2,1)} %param.13) | copy-start | bytes 884740
  299.8 19.1 %copy-start.17 = (f32[1,3072]{1,0:T(1,128)S(1)}, f32[1,3072]{1,0:T(1,128)}, u32[]{:S(2)}) copy-start(f32[1,3072]{1,0:T(1,128)} %copy-done.16) | copy-start | bytes 36868
  318.9 51.6 %copy-start.21 = (f32[48]{0:T(128)S(1)}, f32[48]{0:T(128)}, u32[]{:S(2)}) copy-start(f32[48]{0:T(128)} %copy-done.20) | copy-start | bytes 580
  318.9 51.6 %copy-start.24 = (f32[48]{0:T(128)S(1)}, f32[48]{0:T(128)}, u32[]{:S(2)}) copy-start(f32[48]{0:T(128)} %copy-done.23) | copy-start | bytes 580
  318.9 52.8 %copy-start.11 = (bf16[1,48,3072]{2,1,0:T(8,128)(2,1)S(1)}, bf16[1,48,3072]{2,1,0:T(8,128)(2,1)}, u32[]{:S(2)}) copy-start(bf16[1,48,3072]{2,1,0:T(8,128)(2,1)} %param.19) | copy-start | bytes 884740
  (5 other events, 4.6 us)
Sparse Core Ops, SparseCore 0:
  10.2 62.9 all-gather.8
  74.7 36.1 all-gather.6
  113.7 51.8 all-gather.4
  166.9 80.6 all-gather.10
  298.5 71.9 reduce-scatter.1
where the time goes:
time: 381 us; the launch traced here: 380 us
  waiting for transfers between devices  219 us (57%)
  blocking collectives  59 us (15%)
  local copies, waits for them, and re-layouts  34.1 us (9%)
  matrix products  33.8 us (9%)
  other arithmetic  14.5 us (4%)
  between operations  14.3 us (4%)
  starting transfers between devices  5.89 us (2%)
    all_gather x1, waiting for transfers between devices, on_device(): w_all = lax.all_gather(w_heads, 'cand', axis=2, tiled=True)  75.6 us
    reduce_scatter x1, waiting for transfers between devices, on_device(): lax.psum_scatter(times_transposed(lax.slice_in_dim(d_projected, 0, rows_l...  43.6 us
    all_gather x1, waiting for transfers between devices, on_device(): gathered = lax.all_gather(modulated, 'seq', axis=0, tiled=True)  42.7 us
    all_gather x1, waiting for transfers between devices, on_device(): piece = lax.all_gather(input_weight, 'cand', axis=0, tiled=True)  34.5 us
    all_gather x1, blocking collectives, on_device(): modulation = lax.all_gather(mod_mine, 'seq', axis=1, tiled=True)[0]  31.6 us
    all_gather x1, waiting for transfers between devices, on_device(): w_heads = lax.all_gather(output_weight, 'seq', axis=0, tiled=True)  20.8 us
    all_to_all x1, blocking collectives, on_device(): lax.all_to_all(attended, 'seq', split_axis=0, concat_axis=1, tiled=True)  18.7 us
    dot_general x2, matrix products, times_transposed(): lax.dot_general(left, right, (((1,), (1,)), ((), ())), preferred_element_...  11.9 us
  transfers between devices with their start and end apart: 6, of which 5 were waited for; matrix products, arithmetic and copies ran while one was open for 11% of the time, Pallas kernels for 0%

commit v1 on v0

--- a/solution.py
+++ b/solution.py
@@ -159,7 +159,12 @@
     gathered = lax.all_gather(modulated, "seq", axis=0, tiled=True)
     length = gathered.shape[0]
     tables = rope_tables(positions, HEAD)
-    piece = lax.all_gather(input_weight, "cand", axis=0, tiled=True)
+
+    def open_sources_all(panel):
+        field_out = jnp.stack([panel for _ in range(lax.axis_size("cand"))], axis=0)
+        return jnp.concatenate(lax.all_to_all(field_out, "cand", 0, 0), axis=0)
+
+    piece = open_sources_all(input_weight)
     projected = jnp.dot(
         gathered, piece.reshape(piece.shape[0], group_cols), preferred_element_type=jnp.float32
     )

time: 381 us -> 362 us (0.950)
  waiting for transfers between devices: 219 us -> 173 us
  local copies, waits for them, and re-layouts: 34.1 us -> 56.6 us
  starting transfers between devices: 5.89 us -> 11 us
    all_to_all x0 -> x1, waiting for transfers between devices: none -> 51.8 us  [open_sources_all(): return jnp.concatenate(lax.all_to_all(field_out, 'cand', 0, 0), axis=0)]
    all_gather x1, waiting for transfers between devices: 42.7 us -> 0.01 us  [on_device(): gathered = lax.all_gather(modulated, 'seq', axis=0, tiled=True)]
    all_gather x1, waiting for transfers between devices: 75.6 us -> 40.6 us  [on_device(): w_all = lax.all_gather(w_heads, 'cand', axis=2, tiled=True)]
    all_gather x1, waiting for transfers between devices: 34.5 us -> 15.2 us  [on_device(): lax.all_gather(input_weight, 'cand', axis=0, tiled=True)]
    all_to_all x0 -> x1, local copies, waits for them, and re-layouts: none -> 12.7 us  [open_sources_all(): return jnp.concatenate(lax.all_to_all(field_out, 'cand', 0, 0), axis=0)]
    unnamed x64 -> x40, local copies, waits for them, and re-layouts: 9.31 us -> 16.1 us
    reshape x1 -> x0, local copies, waits for them, and re-layouts: 6.68 us -> none  [on_device(): piece.reshape(piece.shape[0], group_cols)]
    dot_general x0 -> x1, local copies, waits for them, and re-layouts: none -> 6.6 us  [on_device(): jnp.dot(gathered, piece.reshape(piece.shape[0], group_cols), preferred_el...]
  transfers between devices with their start and end apart: 6 -> 7, of which waited for: 5 -> 5; matrix products, arithmetic and copies ran while one was open for 11% -> 20% of each run, Pallas kernels for 0% -> 0%
where the time goes in v1:
time: 362 us; the launch traced here: 360 us
  waiting for transfers between devices  173 us (48%)
  blocking collectives  58.9 us (16%)
  local copies, waits for them, and re-layouts  56.6 us (16%)
  matrix products  35 us (10%)
  between operations  14.1 us (4%)
  starting transfers between devices  11 us (3%)
  other arithmetic  11 us (3%)
    all_to_all x1, waiting for transfers between devices, open_sources_all(): return jnp.concatenate(lax.all_to_all(field_out, 'cand', 0, 0), axis=0)  51.8 us
    reduce_scatter x1, waiting for transfers between devices, on_device(): lax.psum_scatter(times_transposed(lax.slice_in_dim(d_projected, 0, rows_l...  44.1 us
    all_gather x1, waiting for transfers between devices, on_device(): w_all = lax.all_gather(w_heads, 'cand', axis=2, tiled=True)  40.6 us
    all_gather x1, blocking collectives, on_device(): modulation = lax.all_gather(mod_mine, 'seq', axis=1, tiled=True)[0]  31.6 us
    all_gather x1, waiting for transfers between devices, on_device(): w_heads = lax.all_gather(output_weight, 'seq', axis=0, tiled=True)  20.4 us
    all_to_all x1, blocking collectives, on_device(): lax.all_to_all(attended, 'seq', split_axis=0, concat_axis=1, tiled=True)  18.6 us
    unnamed x40, local copies, waits for them, and re-layouts  16.1 us
    all_gather x1, waiting for transfers between devices, on_device(): lax.all_gather(input_weight, 'cand', axis=0, tiled=True)  15.2 us
  transfers between devices with their start and end apart: 7, of which 5 were waited for; matrix products, arithmetic and copies ran while one was open for 20% of the time, Pallas kernels for 0%

profile of v1, /device:TPU:0, one launch (start us, length us, event | category | flops | bytes accessed | tf_op | source)
XLA Modules:
  0.0 360.1 jit_solution(8589201587457308293)
XLA Ops:
  8.6 1.2 dynamic-slice
  10.5 8.7 %all-reduce = bf16[4,1152]{1,0:T(4,128)(2,1)S(1)} all-reduce(bf16[4,1152]{1,0:T(4,128)(2,1)S(1)} %convolution_convert_fusion.2), channel_id=2, replica_groups=mesh['cand'=4,'seq'=8] {'cand'}, use_global_device_ids=true, to_apply=%region_0.1.clone | all-reduce | flops 4608 | bytes 18432
  19.9 31.6 %all_gather.15 = f32[1,9216]{1,0:T(1,128)S(1)} all-gather(f32[1,1152]{1,0:T(1,128)S(1)} %dynamic-slice_convert_fusion), channel_id=1, replica_groups=mesh['cand'=4,'seq'=8] {'seq'}, dimensions={1}, use_global_device_ids=true | all-gather | bytes 41472 | tf_op jit(solution)/shard_map/all_gather | solution.py:152
  52.8 20.4 %all-gather.7.cloned.1.call-done = bf16[16,128,768]{2,1,0:T(8,128)(2,1)} async-done(((bf16[2,128,768]{2,1,0:T(8,128)(2,1)}), bf16[16,128,768]{2,1,0:T(8,128)(2,1)}) %all-gather.7.cloned.1.call-update) | async-done | bytes 3145744 | tf_op jit(solution)/shard_map/all_gather | solution.py:172
  74.6 2.0 copy.74
  76.6 2.5 stack.23
  79.0 5.1 %all-to-all-start = ((bf16[4,768,2,384]{1,3,2,0:T(8,128)(2,1)}), bf16[4,768,2,384]{1,3,2,0:T(8,128)(2,1)}, u32[]{:S(2)}, u32[]{:S(2)}) async-start(bf16[4,768,2,384]{1,3,2,0:T(8,128)(2,1)} %stack.23), calls=%async_computation | async-start | bytes 9437184 | tf_op jit(solution)/shard_map/all_to_all | solution.py:165
  86.2 51.8 %all-to-all-done = bf16[4,768,2,384]{1,3,2,0:T(8,128)(2,1)} async-done(((bf16[4,768,2,384]{1,3,2,0:T(8,128)(2,1)}), bf16[4,768,2,384]{1,3,2,0:T(8,128)(2,1)}, u32[]{:S(2)}, u32[]{:S(2)}) %all-to-all-start) | async-done | bytes 4718624 | tf_op jit(solution)/shard_map/all_to_all | solution.py:165
  138.0 12.7 %copy.75 = bf16[4,768,2,384]{3,2,1,0:T(2,128)(2,1)} copy(bf16[4,768,2,384]{1,3,2,0:T(8,128)(2,1)} %all-to-all-done) | data formatting | bytes 9437184 | tf_op jit(solution)/shard_map/all_to_all | solution.py:165
  150.7 5.3 %copy.115 = bf16[384,8,2,384]{3,1,2,0:T(8,128)(2,1)} copy(bf16[384,8,2,384]{3,2,1,0:T(2,128)(2,1)} %bitcast.148) | data formatting | bytes 9437184
  156.0 6.6 %copy.76 = bf16[768,3072]{1,0:T(8,128)(2,1)} copy(bf16[768,3072]{0,1:T(8,128)(2,1)} %bitcast.149) | data formatting | bytes 9437184 | tf_op jit(solution)/shard_map/dot_general | solution.py:168
  162.6 5.3 %fusion.5 = f32[3,2,384,128]{2,3,0,1:T(8,128)S(1)} fusion(bf16[2,3,128,3072]{3,2,1,0:T(8,128)(2,1)} %bitcast.152, bf16[384,3072]{1,0:T(8,128)(2,1)} %all-gather.5.cloned.1.call-done), kind=kOutput, calls=%fused_computation.13 | convolution fusion | flops 1811939328 | bytes 8257536 | tf_op jit(solution)/shard_map/dot_general | solution.py:168
  168.0 40.6 %all-gather.9.cloned.1.call-done = bf16[16,128,3072]{2,1,0:T(8,128)(2,1)} async-done(((bf16[16,128,768]{2,1,0:T(8,128)(2,1)}), bf16[16,128,3072]{2,1,0:T(8,128)(2,1)}) %all-gather.9.cloned.1.call-update) | async-done | bytes 12582928 | tf_op jit(solution)/shard_map/all_gather | solution.py:173
  208.6 8.5 %convolution_convert_fusion.1 = bf16[48,2048]{1,0:T(8,128)(2,1)S(1)} fusion(bf16[2048,3072]{1,0:T(8,128)(2,1)} %bitcast.146, bf16[1,48,3072]{2,1,0:T(8,128)(2,1)S(1)} %copy-done.8, f32[3072]{0:T(1024)S(1)} %bitcast.160), kind=kOutput, calls=%fused_computation.11 | convolution fusion | flops 604520448 | bytes 13086720 | tf_op jit(solution)/shard_map/dot_general | solution.py:81
  217.8 5.5 %all-to-all-start.2 = ((bf16[48,8,256]{2,0,1:T(8,128)(2,1)}), bf16[48,8,256]{2,0,1:T(8,128)(2,1)}, u32[]{:S(2)}, u32[]{:S(2)}) async-start(bf16[48,8,256]{2,0,1:T(8,128)(2,1)} %bitcast.145), calls=%async_computation.2 | async-start | bytes 393216 | tf_op jit(solution)/shard_map/all_to_all | solution.py:180
  225.7 2.0 gather_fusion.1
  227.7 2.8 gather_fusion
  230.5 1.8 fusion.31
  232.3 15.2 %all-gather.11.cloned.1.call-done = bf16[3072,2,384]{2,1,0:T(2,128)(2,1)} async-done(((bf16[768,2,384]{2,1,0:T(2,128)(2,1)}), bf16[3072,2,384]{2,1,0:T(2,128)(2,1)}) %all-gather.11.cloned.1.call-update) | async-done | bytes 4718608 | tf_op jit(solution)/shard_map/all_gather | solution.py:182
  247.5 5.3 %copy.116 = bf16[384,8,2,384]{3,1,2,0:T(8,128)(2,1)} copy(bf16[384,8,2,384]{3,2,1,0:T(2,128)(2,1)} %bitcast.150) | data formatting | bytes 9437184
  253.8 1.5 fusion.45
  255.3 1.9 multiply_reduce_fusion
  261.8 2.7 gather_fusion.2
  264.5 2.1 copy.95
  266.6 2.7 gather_fusion.3
  269.4 1.4 multiply_reduce_fusion.2
  271.9 5.8 %convolution_convert_fusion = bf16[384,3072]{1,0:T(8,128)(2,1)} fusion(bf16[384,768]{0,1:T(8,128)(2,1)S(1)} %bitcast.156, bf16[3072,768]{1,0:T(8,128)(2,1)} %bitcast.151), kind=kOutput, calls=%fused_computation.4 | convolution fusion | flops 1813118976 | bytes 7667712 | tf_op jit(solution)/shard_map/dot_general | solution.py:81
  277.8 1.4 fusion.10
  279.5 18.6 %all_to_all.37 = bf16[8,48,256]{2,1,0:T(8,128)(2,1)S(1)} all-to-all(bf16[8,48,256]{2,1,0:T(8,128)(2,1)S(1)} %convert_element_type.131), channel_id=1, replica_groups=mesh['cand'=4,'seq'=8] {'seq'}, dimensions={0} | all-to-all | bytes 393216 | tf_op jit(solution)/shard_map/all_to_all | solution.py:175
  298.2 8.0 %fusion.2 = bf16[1,48,3072]{2,1,0:T(8,128)(2,1)} fusion(bf16[48,2048]{1,0:T(8,128)(2,1)S(1)} %bitcast.153, bf16[2048,3072]{1,0:T(8,128)(2,1)} %bitcast.147, bf16[1,48,3072]{2,1,0:T(8,128)(2,1)S(1)} %copy-done.2, f32[3072]{0:T(1024)S(1)} %bitcast.161), kind=kOutput, calls=%fused_computation.8 | convolution fusion | flops 604569600 | bytes 13381632 | tf_op jit(solution)/shard_map/dot_general | solution.py:176
  306.2 44.1 %reduce-scatter.2.cloned.1.call-done = bf16[48,3072]{1,0:T(8,128)(2,1)} async-done(((bf16[384,3072]{1,0:T(8,128)(2,1)}), bf16[48,3072]{1,0:T(8,128)(2,1)}) %reduce-scatter.2.cloned.1.call-update) | async-done | bytes 294928 | tf_op jit(solution)/shard_map/reduce_scatter | solution.py:183
  351.5 2.0 fusion.24
  (91 shorter events, 18.8 us)
Async XLA Ops:
  7.2 3.0 copy-start
  7.2 44.2 %copy-start.2 = (bf16[1,48,3072]{2,1,0:T(8,128)(2,1)S(1)}, bf16[1,48,3072]{2,1,0:T(8,128)(2,1)}, u32[]{:S(2)}) copy-start(bf16[1,48,3072]{2,1,0:T(8,128)(2,1)} %param.13) | copy-start | bytes 884740
  7.2 66.1 %all-gather.7.cloned.1.call-start = ((), (), s32[]{:S(2)}) async-start(), calls=%async_computation.5 | async-start | bytes 3538944 | tf_op jit(solution)/shard_map/all_gather | solution.py:172
  7.9 154.7 %all-gather.5.cloned.1.call-start = ((), (), s32[]{:S(2)}) async-start(), calls=%async_computation.4 | async-start | bytes 2654208 | tf_op jit(solution)/shard_map/all_gather | solution.py:159
  52.8 155.8 %all-gather.9.cloned.1.call-start = ((), (), s32[]{:S(2)}) async-start(), calls=%async_computation.6 | async-start | bytes 15728640 | tf_op jit(solution)/shard_map/all_gather | solution.py:173
  73.3 1.3 copy-start.5
  73.3 174.2 %all-gather.11.cloned.1.call-start = ((), (), s32[]{:S(2)}) async-start(), calls=%async_computation.7 | async-start | bytes 5898240 | tf_op jit(solution)/shard_map/all_gather | solution.py:182
  79.0 5.2 %copy-start.16 = (s32[3,384]{1,0:T(4,128)S(1)}, s32[3,384]{1,0:T(4,128)}, u32[]{:S(2)}) copy-start(s32[3,384]{1,0:T(4,128)} %param.15) | copy-start | bytes 13828
  79.0 5.7 %copy-start.17 = (s32[128]{0:T(128)S(1)}, s32[128]{0:T(128)}, u32[]{:S(2)}) copy-start(s32[128]{0:T(128)} %constant.69) | copy-start | bytes 1540
  79.0 59.0 %all-to-all-start = ((bf16[4,768,2,384]{1,3,2,0:T(8,128)(2,1)}), bf16[4,768,2,384]{1,3,2,0:T(8,128)(2,1)}, u32[]{:S(2)}, u32[]{:S(2)}) async-start(bf16[4,768,2,384]{1,3,2,0:T(8,128)(2,1)} %stack.23), calls=%async_computation | async-start | bytes 9437184 | tf_op jit(solution)/shard_map/all_to_all | solution.py:165
  162.6 46.0 %copy-start.8 = (bf16[1,48,3072]{2,1,0:T(8,128)(2,1)S(1)}, bf16[1,48,3072]{2,1,0:T(8,128)(2,1)}, u32[]{:S(2)}) copy-start(bf16[1,48,3072]{2,1,0:T(8,128)(2,1)} %param.19) | copy-start | bytes 884740
  167.9 85.9 %copy-start.3 = (f32[3,2,384,128]{2,3,0,1:T(8,128)}, f32[3,2,384,128]{2,3,0,1:T(8,128)S(1)}, u32[]{:S(2)}) copy-start(f32[3,2,384,128]{2,3,0,1:T(8,128)S(1)} %fusion.5) | copy-start | bytes 3538948
  217.8 35.0 %all-to-all-start.2 = ((bf16[48,8,256]{2,0,1:T(8,128)(2,1)}), bf16[48,8,256]{2,0,1:T(8,128)(2,1)}, u32[]{:S(2)}, u32[]{:S(2)}) async-start(bf16[48,8,256]{2,0,1:T(8,128)(2,1)} %bitcast.145), calls=%async_computation.2 | async-start | bytes 393216 | tf_op jit(solution)/shard_map/all_to_all | solution.py:180
  223.3 127.0 %reduce-scatter.2.cloned.1.call-start = ((), (), s32[]{:S(2)}) async-start(), calls=%async_computation.8 | async-start | bytes 2654208 | tf_op jit(solution)/shard_map/reduce_scatter | solution.py:183
  224.6 5.9 %copy-start.15 = (f32[128]{0:T(128)S(1)}, f32[128]{0:T(128)}, u32[]{:S(2)}) copy-start(f32[128]{0:T(128)} %constant.63.clone) | copy-start | bytes 1540
  232.3 23.0 %copy-start.11 = (bf16[2,384,128]{1,2,0:T(8,128)(2,1)}, bf16[2,384,128]{1,2,0:T(8,128)(2,1)S(1)}, u32[]{:S(2)}) copy-start(bf16[2,384,128]{1,2,0:T(8,128)(2,1)S(1)} %get-tuple-element.14) | copy-start | bytes 589828
  252.8 2.5 copy-start.13
  257.1 1.3 copy-start.4
  258.6 0.9 copy-start.12
  258.6 1.0 copy-start.14
  269.4 1.4 copy-start.6
  269.4 1.4 copy-start.7
  270.8 0.9 copy-start.10
  298.1 53.4 %copy-start.9 = (bf16[1,48,3072]{2,1,0:T(8,128)(2,1)S(1)}, bf16[1,48,3072]{2,1,0:T(8,128)(2,1)}, u32[]{:S(2)}) copy-start(bf16[1,48,3072]{2,1,0:T(8,128)(2,1)} %param.19) | copy-start | bytes 884740
  298.1 55.4 %copy-start.1 = (bf16[768,1152]{1,0:T(8,128)(2,1)S(1)}, bf16[768,1152]{1,0:T(8,128)(2,1)}, u32[]{:S(2)}) copy-start(bf16[768,1152]{1,0:T(8,128)(2,1)} %param.16) | copy-start | bytes 5308420
Sparse Core Ops, SparseCore 0:
  10.2 63.0 all-gather.6
  76.0 50.3 all-gather.4
  128.0 80.5 all-gather.8
  210.0 37.4 all-gather.10
  277.9 72.3 reduce-scatter.1
